TPU v7x, 128 devices: a whole 4x4x4 slice. The times are simulated.
128 devices in a mesh: row: 16 (over y_hi, z, core), col: 8 (over x, y_lo).
Axes of the slice: x: 4, y: 4 (y_hi: 2, y_lo: 2; y = y_hi * 2 + y_lo), z: 4, core: 2. Of those that a mesh axis runs over, the one named last changes fastest.
Arguments:
- cells: float32 [4096, 1024], P(('row', 'col')), may hold values from 0 to 1
- instance_cell: int32 [64, 256], P('row', 'col'), may hold values from 0 to 4095, as said below
- target: float32 [2048, 8192], P('row', 'col'), may hold values from 0 to 1
- row_taps: float32 [8, 65], replicated, may hold values from -0.75 to 0.75
- col_taps: float32 [8, 65], replicated, may hold values from -0.75 to 0.75
- kernel_weight: float32 [8], replicated, may hold values from 0.05 to 0.5
Outputs:
- cells_out: float32 [4096, 1024], P(('row', 'col'))
Inputs may be any that keep to these rules, and one draw needn't show every extreme that they name: `instance_cell`: each entry is the index of the device that holds the cell, along row+col with row slowest, times 32, plus the cell's place there. Tile (a, b) lies on device (a // 4, b // 32). Among one device's tiles at most 2 name cells held by any one device, and one holding device is named by exactly 2 tiles of every device.
All inputs are finite; a program needn't handle non-finite values.
Results may differ from a plain program's by a relative error of at most 0.00016.
Values sent between devices are 32-bit elements; how exact they have to be, the bound alone decides.
A program may use at most 128 MiB of HBM per device.

v0:
```python
import functools

import jax
import jax.numpy as jnp
from jax import lax
from jax.experimental import pallas as pl
from jax.experimental.pallas import tpu as pltpu
from jax.sharding import PartitionSpec as P

TILE = 32
TAPS = 65
KERNELS = 8
ROWS = 128
COLS = 1024
TILE_ROWS = 4
TILE_COLS = 32
TILES = 128
SLOTS = 32
WIDE = 36
GROUPS = 9
STEEPNESS = 4.0
THRESHOLD = 0.3
STEP_RATE = 0.5
MESH = pl.DeviceIdType.MESH
BF16 = jnp.bfloat16
F32 = jnp.float32
I32 = jnp.int32
WHOLE = pl.BlockSpec(memory_space=pltpu.VMEM)
SCALARS = pl.BlockSpec(memory_space=pltpu.SMEM)

NEIGHBOURS = tuple((dr, dc) for dr in (-1, 0, 1) for dc in (-1, 0, 1) if (dr, dc) != (0, 0))


def span(step, count, inside):
    if step == 0:
        return pl.ds(1, count)
    if step < 0:
        return pl.ds(1 if inside else 0, 1)
    return pl.ds(count if inside else count + 1, 1)


def split(value):
    high = value.astype(BF16)
    return high, (value - high.astype(F32)).astype(BF16)


def mm(a, b):
    return jnp.dot(a, b, preferred_element_type=F32)


def swap_blocks(vectors):
    lane = lax.broadcasted_iota(I32, vectors[0].shape, 2)
    low = lane < 64
    even = (lane & 32) == 0
    a, b, c, d = vectors
    a, c = (
        jnp.where(low, a, pltpu.roll(c, 64, 2)),
        jnp.where(low, pltpu.roll(a, 64, 2), c),
    )
    b, d = (
        jnp.where(low, b, pltpu.roll(d, 64, 2)),
        jnp.where(low, pltpu.roll(b, 64, 2), d),
    )
    a, b = (
        jnp.where(even, a, pltpu.roll(b, 32, 2)),
        jnp.where(even, pltpu.roll(a, 96, 2), b),
    )
    c, d = (
        jnp.where(even, c, pltpu.roll(d, 32, 2)),
        jnp.where(even, pltpu.roll(c, 96, 2), d),
    )
    return a, b, c, d


def bands_kernel(row_taps, col_taps, a_hi, a_lo, at_hi, at_lo, b_both, bt_both, pad):
    pad[...] = jnp.zeros_like(pad)
    pad[0:8, 0:TAPS] = row_taps[...]
    pad[8:16, 0:TAPS] = col_taps[...]
    c = lax.broadcasted_iota(I32, (256, 256), 0)
    p = lax.broadcasted_iota(I32, (256, 256), 1)
    placed = (c & ~31) + ((c & 3) << 3) + ((c & 31) >> 2)
    permute = (p == placed).astype(F32).astype(BF16)

    def shifted(line):
        row = pad[pl.ds(line, 1), :]
        return pltpu.roll(jnp.broadcast_to(row, (128, 256)), 0, 1, stride=1, stride_axis=0)

    for k in range(KERNELS):
        rows = pl.ds(k * 128, 128)
        for part, a_out, at_out in zip(split(shifted(k)), (a_hi, a_lo), (at_hi, at_lo)):
            ordered = mm(part, permute)
            a_out[rows, :] = ordered.astype(BF16)
            at_out[:, rows] = ordered.T.astype(BF16)
        for i, part in enumerate(split(shifted(8 + k))):
            part = part.astype(F32)
            lanes = pl.ds(i * 128, 128)
            b_both[k, :, lanes] = part.T.astype(BF16)
            bt_both[k, 0:128, lanes] = part[:, 128:256].astype(BF16)
            bt_both[k, 128:256, lanes] = part[:, 0:128].astype(BF16)


def image_kernel(
    weight, wide, target, a_hi, a_lo, at_hi, at_lo, b_both, bt_both, out,
    x_hi, x_lo, y_hi, y_lo, fields, p_hi, p_lo, q_hi, q_lo,
):
    x_hi[192:256, :] = jnp.zeros((64, GROUPS * 128), BF16)
    x_lo[192:256, :] = jnp.zeros((64, GROUPS * 128), BF16)
    for g in range(GROUPS):
        turned = swap_blocks([wide[:, 4 * g + q] for q in range(4)])
        value = jnp.concatenate(turned, axis=1).reshape(192, 128)
        lanes = pl.ds(g * 128, 128)
        x_hi[0:192, lanes], x_lo[0:192, lanes] = split(value)
    for g in range(GROUPS):
        lanes = pl.ds(g * 128, 128)
        high, low = x_hi[:, lanes], x_lo[:, lanes]
        both = mm(a_hi[...], jnp.concatenate([high, low], axis=1))
        value = both[:, :128] + both[:, 128:] + mm(a_lo[...], high)
        y_hi[:, g], y_lo[:, g] = (v.reshape(KERNELS, 128, 128) for v in split(value))
    intensity = jnp.zeros((1024, 128), F32)
    for k in range(KERNELS):
        def window(ref):
            return jnp.concatenate(
                [ref[k, 0:8].reshape(1024, 128), ref[k, 1:9].reshape(1024, 128)], axis=1
            )
        both = mm(window(y_hi), b_both[k])
        field = both[:, :128] + both[:, 128:] + mm(window(y_lo), b_both[k, :, 0:128])
        fields[k] = field
        intensity = intensity + weight[k] * field * field
    wanted = jnp.concatenate([target[:, 128 * n:128 * n + 128] for n in range(8)], axis=0)
    resist = 1.0 / (1.0 + jnp.exp(-STEEPNESS * (intensity - THRESHOLD)))
    sensitivity = 2.0 * (resist - wanted) * STEEPNESS * resist * (1.0 - resist)
    for ref in (p_hi, p_lo):
        ref[0] = jnp.zeros((128, 128), BF16)
        ref[9] = jnp.zeros((128, 128), BF16)
    for k in range(KERNELS):
        product = (2.0 * weight[k]) * sensitivity * fields[k]
        p_hi[1:9], p_lo[1:9] = (v.reshape(8, 128, 128) for v in split(product))

        def window(ref):
            return jnp.concatenate(
                [ref[0:9].reshape(1152, 128), ref[1:10].reshape(1152, 128)], axis=1
            )
        both = mm(window(p_hi), bt_both[k])
        value = both[:, :128] + both[:, 128:] + mm(window(p_lo), bt_both[k, :, 0:128])
        high, low = split(value)
        for g in range(GROUPS):
            lanes = pl.ds(g * 128, 128)
            rows = pl.ds(k * 128, 128)
            q_hi[rows, lanes] = high[128 * g:128 * g + 128]
            q_lo[rows, lanes] = low[128 * g:128 * g + 128]
    for g in range(GROUPS):
        lanes = pl.ds(g * 128, 128)
        high, low = q_hi[:, lanes], q_lo[:, lanes]
        both = mm(at_hi[0:192, :], jnp.concatenate([high, low], axis=1))
        value = both[:, :128] + both[:, 128:] + mm(at_lo[0:192, :], high)
        value = value.reshape(6, 32, 128)
        turned = swap_blocks([value[:, 8 * s:8 * s + 8] for s in range(4)])
        for q in range(4):
            out[:, 4 * g + q] = turned[q]


def place(mesh_shape):
    row_count, col_count = mesh_shape
    row, col = lax.axis_index("row"), lax.axis_index("col")
    return row_count, col_count, row, col, row * col_count + col


def everyone(total, col_count, me, body):
    def step(i, carry):
        peer = lax.rem(me + i, total)
        body(peer, (peer // col_count, lax.rem(peer, col_count)))
        return carry
    lax.fori_loop(1, total, step, 0)


def greet_all(total, col_count, me):
    barrier = pltpu.get_barrier_semaphore()

    def signal(peer, where):
        pl.semaphore_signal(barrier, inc=1, device_id=where, device_id_type=MESH)
    everyone(total, col_count, me, signal)
    return barrier


def exists(coords, counts):
    ok = None
    for at, count, step in coords:
        if step == 0:
            continue
        here = (at + step >= 0) if step < 0 else (at + step < count)
        ok = here if ok is None else jnp.logical_and(ok, here)
    return ok


def fetch_kernel(
    mesh_shape, inst, cells, wide, tile_of, selected,
    pad, mine, table, cells3, outgoing, arrived, index_v, index_s, where_v, where_s,
    table_send, table_recv, cell_send, cell_recv, halo_send, halo_recv, local,
):
    row_count, col_count, row, col, me = place(mesh_shape)
    total = row_count * col_count
    for a in (0, 5):
        wide[a] = jnp.zeros((WIDE, 8, 128), F32)
    for b in (0, 33, 34, 35):
        wide[1:5, b] = jnp.zeros((TILE_ROWS, 8, 128), F32)
    barrier = greet_all(total, col_count, me)
    pad[...] = jnp.zeros_like(pad)
    pad[0:TILE_ROWS, 0:TILE_COLS] = inst[...]
    lines = pad[...]
    line = lax.broadcasted_iota(I32, lines.shape, 0)
    flat = jnp.zeros((8, 128), I32)
    for a in range(TILE_ROWS):
        moved = pltpu.roll(lines, 32 * a, 1) if a else lines
        flat = flat + jnp.where(line == a, moved, 0)
    flat = jnp.sum(flat, axis=0, keepdims=True)
    mine[0] = flat
    table[me] = flat
    for r in range(8):
        cells3[:, r, :] = cells[:, 128 * r:128 * r + 128]
    pl.semaphore_wait(barrier, total - 1)

    def send_table(peer, where):
        pltpu.make_async_remote_copy(
            src_ref=mine, dst_ref=table.at[pl.ds(me, 1)], send_sem=table_send, recv_sem=table_recv,
            device_id=where, device_id_type=MESH,
        ).start()
    everyone(total, col_count, me, send_table)

    lane = lax.broadcasted_iota(I32, (128, 128), 1)
    sub = lax.broadcasted_iota(I32, (128, 128), 0)
    diagonal = lane == sub

    def as_row(column):
        return jnp.sum(jnp.where(diagonal, column, 0), axis=0, keepdims=True)
    owner = flat >> 5
    held = owner == sub
    first = jnp.min(jnp.where(held, lane, TILES), axis=1, keepdims=True)
    last = jnp.max(jnp.where(held, lane, -1), axis=1, keepdims=True)
    second = jnp.sum(jnp.where(held & (lane != first), 1, 0), axis=0, keepdims=True)
    tile_of[0:1, :] = as_row(jnp.minimum(first, TILES - 1))
    tile_of[1:2, :] = as_row(jnp.maximum(last, 0))
    where_v[...] = owner * 2 + second
    where_copy = pltpu.make_async_copy(where_v, where_s, local.at[0])
    where_copy.start()

    others = pl.ds(0, total - 1)
    neighbour = (lax.rem(row + 1, row_count), col)
    arrival = pltpu.make_async_remote_copy(
        src_ref=table.at[others], dst_ref=table.at[others], send_sem=table_send, recv_sem=table_recv,
        device_id=neighbour, device_id_type=MESH,
    )
    arrival.wait()

    asked = table[...].reshape(128, 128)
    hit = (asked >> 5) == me
    key = lane * SLOTS + (asked & (SLOTS - 1))
    first = jnp.min(jnp.where(hit, key, TILES * SLOTS), axis=1, keepdims=True)
    last = jnp.max(jnp.where(hit, key, -1), axis=1, keepdims=True)
    chosen = (
        as_row(jnp.where(first < TILES * SLOTS, first & (SLOTS - 1), -1)),
        as_row(jnp.where(last > first, last & (SLOTS - 1), -1)),
    )
    for s in range(2):
        selected[s:s + 1, :] = chosen[s]
        index_v[s:s + 1, :] = jnp.maximum(chosen[s], 0)
    index_copy = pltpu.make_async_copy(index_v, index_s, local.at[1])
    index_copy.start()
    index_copy.wait()

    def send_cells(peer, where):
        for s in range(2):
            outgoing[2 * peer + s] = cells3[index_s[s, peer]]
        pltpu.make_async_remote_copy(
            src_ref=outgoing.at[pl.ds(2 * peer, 2)], dst_ref=arrived.at[pl.ds(2 * me, 2)],
            send_sem=cell_send, recv_sem=cell_recv, device_id=where, device_id_type=MESH,
        ).start()
    everyone(total, col_count, me, send_cells)
    for s in range(2):
        arrived[2 * me + s] = cells3[index_s[s, me]]
    where_copy.wait()
    others = pl.ds(0, 2 * (total - 1))
    pltpu.make_async_remote_copy(
        src_ref=outgoing.at[others], dst_ref=arrived.at[others], send_sem=cell_send, recv_sem=cell_recv,
        device_id=neighbour, device_id_type=MESH,
    ).wait()

    def put(t, carry):
        wide[1 + t // TILE_COLS, 1 + lax.rem(t, TILE_COLS)] = arrived[where_s[0, t]]
        return carry
    lax.fori_loop(0, TILES, put, 0)

    def halo(i, dr, dc):
        return pltpu.make_async_remote_copy(
            src_ref=wide.at[span(dr, TILE_ROWS, True), span(dc, TILE_COLS, True)],
            dst_ref=wide.at[span(-dr, TILE_ROWS, False), span(-dc, TILE_COLS, False)],
            send_sem=halo_send.at[i], recv_sem=halo_recv.at[i],
            device_id=(row + dr, col + dc), device_id_type=MESH,
        )
    exchange(halo, row_count, col_count, row, col)


def exchange(halo, row_count, col_count, row, col):
    for i, (dr, dc) in enumerate(NEIGHBOURS):
        @pl.when(exists(((row, row_count, dr), (col, col_count, dc)), None))
        def _():
            halo(i, dr, dc).start()
    for i, (dr, dc) in enumerate(NEIGHBOURS):
        @pl.when(exists(((row, row_count, dr), (col, col_count, dc)), None))
        def _():
            halo(i, dr, dc).wait_send()

        @pl.when(exists(((row, row_count, -dr), (col, col_count, -dc)), None))
        def _():
            halo(i, dr, dc).wait_recv()


def return_kernel(
    mesh_shape, tile_of, grad, selected, cells, out,
    halo_row, halo_col, halo_corner, own, outgoing, back,
    send, recv, halo_send, halo_recv,
):
    row_count, col_count, row, col, me = place(mesh_shape)
    total = row_count * col_count
    for ref in (halo_row, halo_col, halo_corner):
        ref[...] = jnp.zeros_like(ref)
    barrier = greet_all(total, col_count, me)
    own[...] = grad[1:5, 1:33].reshape(TILES, 8, 128)
    pl.semaphore_wait(barrier, total - 1)

    def halo(i, dr, dc):
        if dr == 0:
            source = grad.at[pl.ds(1, TILE_ROWS), 0 if dc < 0 else TILE_COLS + 1]
            target = halo_col.at[0 if dc < 0 else 1]
        elif dc == 0:
            source = grad.at[0 if dr < 0 else TILE_ROWS + 1, pl.ds(1, TILE_COLS)]
            target = halo_row.at[0 if dr < 0 else 1]
        else:
            source = grad.at[0 if dr < 0 else TILE_ROWS + 1, 0 if dc < 0 else TILE_COLS + 1]
            target = halo_corner.at[2 * (dr > 0) + (dc > 0)]
        return pltpu.make_async_remote_copy(
            src_ref=source, dst_ref=target, send_sem=halo_send.at[i], recv_sem=halo_recv.at[i],
            device_id=(row + dr, col + dc), device_id_type=MESH,
        )
    exchange(halo, row_count, col_count, row, col)
    own[96:128] = own[96:128] + halo_row[0]
    own[0:32] = own[0:32] + halo_row[1]
    for a in range(TILE_ROWS):
        t = TILE_COLS * a
        own[t + 31] = own[t + 31] + halo_col[0, a]
        own[t] = own[t] + halo_col[1, a]
    for i, t in enumerate((127, 96, 31, 0)):
        own[t] = own[t] + halo_corner[i]

    def send_grads(peer, where):
        for s in range(2):
            outgoing[2 * peer + s] = own[tile_of[s, peer]]
        pltpu.make_async_remote_copy(
            src_ref=outgoing.at[pl.ds(2 * peer, 2)], dst_ref=back.at[pl.ds(2 * me, 2)],
            send_sem=send, recv_sem=recv, device_id=where, device_id_type=MESH,
        ).start()
    everyone(total, col_count, me, send_grads)
    for s in range(2):
        back[2 * me + s] = own[tile_of[s, me]]
    cell = lax.broadcasted_iota(I32, (SLOTS, 128), 0)
    selector = jnp.concatenate(
        [(cell == selected[s:s + 1, :]).astype(F32).astype(BF16) for s in range(2)], axis=1
    )
    others = pl.ds(0, 2 * (total - 1))
    pltpu.make_async_remote_copy(
        src_ref=outgoing.at[others], dst_ref=back.at[others], send_sem=send, recv_sem=recv,
        device_id=(lax.rem(row + 1, row_count), col), device_id_type=MESH,
    ).wait()
    flat = back.reshape(2 * TILES * 8, 128)
    for r in range(8):
        value = jnp.concatenate(
            [flat[pl.ds(8 * s + r, 128, stride=16), :] for s in range(2)], axis=0
        )
        high, low = split(value)
        tail = (value - high.astype(F32) - low.astype(F32)).astype(BF16)
        parts = mm(selector, jnp.concatenate([high, low, tail], axis=1))
        total_r = parts[:, 0:128] + parts[:, 128:256] + parts[:, 256:384]
        lanes = slice(128 * r, 128 * r + 128)
        out[:, lanes] = cells[:, lanes] - STEP_RATE * total_r


def shards(mesh_shape, cells, instance_cell, target, row_taps, col_taps, kernel_weight):
    sds = jax.ShapeDtypeStruct
    vmem = pltpu.VMEM
    dma = pltpu.SemaphoreType.DMA
    bands = pl.pallas_call(
        bands_kernel,
        name="bands",
        out_shape=(
            sds((1024, 256), BF16), sds((1024, 256), BF16),
            sds((256, 1024), BF16), sds((256, 1024), BF16),
            sds((8, 256, 256), BF16), sds((8, 256, 256), BF16),
        ),
        in_specs=[WHOLE] * 2,
        out_specs=(WHOLE,) * 6,
        scratch_shapes=[vmem((16, 256), F32)],
    )(row_taps, col_taps)
    wide, tile_of, selected = pl.pallas_call(
        functools.partial(fetch_kernel, mesh_shape),
        name="fetch",
        out_shape=(sds((6, WIDE, 8, 128), F32), sds((2, 128), I32), sds((2, 128), I32)),
        in_specs=[WHOLE] * 2,
        out_specs=(WHOLE,) * 3,
        scratch_shapes=[
            vmem((8, 128), I32), vmem((1, 1, 128), I32), vmem((128, 1, 128), I32),
            vmem((SLOTS, 8, 128), F32), vmem((256, 8, 128), F32), vmem((256, 8, 128), F32),
            vmem((2, 128), I32), pltpu.SMEM((2, 128), I32), vmem((1, 128), I32), pltpu.SMEM((1, 128), I32),
            dma, dma, dma, dma, dma((8,)), dma((8,)), dma((2,)),
        ],
        compiler_params=pltpu.CompilerParams(collective_id=0, has_side_effects=True),
    )(instance_cell, cells)
    grad = pl.pallas_call(
        image_kernel,
        name="image",
        out_shape=sds((6, WIDE, 8, 128), F32),
        in_specs=[SCALARS] + [WHOLE] * 8,
        out_specs=WHOLE,
        scratch_shapes=[
            vmem((256, 1152), BF16), vmem((256, 1152), BF16),
            vmem((8, 9, 128, 128), BF16), vmem((8, 9, 128, 128), BF16),
            vmem((8, 1024, 128), F32),
            vmem((10, 128, 128), BF16), vmem((10, 128, 128), BF16),
            vmem((1024, 1152), BF16), vmem((1024, 1152), BF16),
        ],
    )(kernel_weight, wide, target, *bands)
    return pl.pallas_call(
        functools.partial(return_kernel, mesh_shape),
        name="give",
        out_shape=sds((SLOTS, 1024), F32),
        in_specs=[SCALARS] + [WHOLE] * 3,
        out_specs=WHOLE,
        scratch_shapes=[
            vmem((2, 32, 8, 128), F32), vmem((2, 4, 8, 128), F32), vmem((4, 8, 128), F32),
            vmem((TILES, 8, 128), F32), vmem((256, 8, 128), F32), vmem((256, 8, 128), F32),
            dma, dma, dma((8,)), dma((8,)),
        ],
        compiler_params=pltpu.CompilerParams(collective_id=1, has_side_effects=True),
    )(tile_of, grad, selected, cells)


def solution(mesh):
    placed = (P(("row", "col"), None), P("row", "col"), P("row", "col"), P(), P(), P())
    return jax.shard_map(
        functools.partial(shards, (mesh.shape["row"], mesh.shape["col"])),
        mesh=mesh, in_specs=placed, out_specs=P(("row", "col"), None), check_vma=False,
    )
```

profile of v0, /device:TPU:1, one launch (start us, length us, event | category | flops | bytes accessed | tf_op | source)
XLA Modules:
  0.0 94.5 jit_solution(14840724873520498652)
XLA Ops:
  0.0 42.4 %fetch.1 = (f32[6,36,8,128]{3,2,1,0:T(8,128)}, s32[2,128]{1,0:T(2,128)}, s32[2,128]{1,0:T(2,128)}) custom-call(s32[4,32]{1,0:T(4,128)} %inst.1, f32[32,1024]{1,0:T(8,128)} %cells.3), custom_call_target="tpu_custom_call" | custom-call | tf_op jit(solution)/shard_map/fetch/pallas_call | solution.py:402
  42.5 3.5 %bands.1 = (bf16[1024,256]{1,0:T(8,128)(2,1)}, bf16[1024,256]{1,0:T(8,128)(2,1)}, bf16[256,1024]{1,0:T(8,128)(2,1)}, bf16[256,1024]{1,0:T(8,128)(2,1)}, bf16[8,2...) custom-call(f32[8,65]{1,0:T(8,128)} %row_taps.1, f32[8,65]{1,0:T(8,128)} %col_taps.1), custom_call_target="tpu_custom_call" | custom-call | tf_op jit(solution)/shard_map/bands/pallas_call | solution.py:390
  46.0 13.9 %image.1.grad = f32[6,36,8,128]{3,2,1,0:T(8,128)} custom-call(f32[8]{0:T(128)} %weight.1, f32[6,36,8,128]{3,2,1,0:T(8,128)} %get-tuple-element.15.wide, f32[128,1024]{1,0:T(8,128)} %target.1, bf16[1024,256]{1,0:T(8,128)(2,1)} %get-tuple-element.16.a_hi, bf16[1024,256]{1,0:T(8,128)(2,1)} %get-tuple-element.17.a_lo, ...), custom_call_target="tpu_custom_call" | custom-call | tf_op jit(solution)/shard_map/image/pallas_call | solution.py:416
  59.9 33.0 %give.1 = f32[32,1024]{1,0:T(8,128)} custom-call(s32[2,128]{1,0:T(2,128)} %get-tuple-element.14.tile_of, f32[6,36,8,128]{3,2,1,0:T(8,128)} %image.1.grad, s32[2,128]{1,0:T(2,128)} %get-tuple-element.22.selected, f32[32,1024]{1,0:T(8,128)} %cells.3), custom_call_target="tpu_custom_call" | custom-call | tf_op jit(solution)/shard_map/give/pallas_call | solution.py:430
  92.9 1.6 %copy.8 = f32[32,1024]{1,0:T(8,128)} copy(f32[32,1024]{1,0:T(8,128)} %give.1) | data formatting | bytes 262144
where the time goes:
time: 94.7 us; the launch traced here: 94.5 us
  Pallas kernels  92.9 us (98%)
  local copies, waits for them, and re-layouts  1.57 us (2%)
    pallas_call x1, Pallas kernels, shards(): pl.pallas_call(functools.partial(fetch_kernel, mesh_shape), name='fetch',...  42.4 us
    pallas_call x1, Pallas kernels, shards(): pl.pallas_call(functools.partial(return_kernel, mesh_shape), name='give',...  33 us
    pallas_call x1, Pallas kernels, shards(): pl.pallas_call(image_kernel, name='image', out_shape=sds((6, WIDE, 8, 128...  13.9 us
    pallas_call x1, Pallas kernels, shards(): pl.pallas_call(bands_kernel, name='bands', out_shape=(sds((1024, 256), BF...  3.53 us

commit v1 on v0

v1 whole, which is shorter than its diff:
```python
import functools
import itertools

import jax
import jax.numpy as jnp
from jax import lax
from jax.experimental import pallas as pl
from jax.experimental.pallas import tpu as pltpu
from jax.sharding import PartitionSpec as P

TILE = 32
TAPS = 65
KERNELS = 8
ROWS = 128
COLS = 1024
TILE_ROWS = 4
TILE_COLS = 32
TILES = 128
SLOTS = 32
WIDE = 36
GROUPS = 9
STEEPNESS = 4.0
THRESHOLD = 0.3
STEP_RATE = 0.5
MESH = pl.DeviceIdType.MESH
BF16 = jnp.bfloat16
F32 = jnp.float32
I32 = jnp.int32
WHOLE = pl.BlockSpec(memory_space=pltpu.VMEM)
SCALARS = pl.BlockSpec(memory_space=pltpu.SMEM)

NEIGHBOURS = tuple((dr, dc) for dr in (-1, 0, 1) for dc in (-1, 0, 1) if (dr, dc) != (0, 0))


def span(step, count, inside):
    if step == 0:
        return pl.ds(1, count)
    if step < 0:
        return pl.ds(1 if inside else 0, 1)
    return pl.ds(count if inside else count + 1, 1)


def split(value):
    high = value.astype(BF16)
    return high, (value - high.astype(F32)).astype(BF16)


def mm(a, b):
    return jnp.dot(a, b, preferred_element_type=F32)


def swap_blocks(vectors):
    lane = lax.broadcasted_iota(I32, vectors[0].shape, 2)
    low = lane < 64
    even = (lane & 32) == 0
    a, b, c, d = vectors
    a, c = (
        jnp.where(low, a, pltpu.roll(c, 64, 2)),
        jnp.where(low, pltpu.roll(a, 64, 2), c),
    )
    b, d = (
        jnp.where(low, b, pltpu.roll(d, 64, 2)),
        jnp.where(low, pltpu.roll(b, 64, 2), d),
    )
    a, b = (
        jnp.where(even, a, pltpu.roll(b, 32, 2)),
        jnp.where(even, pltpu.roll(a, 96, 2), b),
    )
    c, d = (
        jnp.where(even, c, pltpu.roll(d, 32, 2)),
        jnp.where(even, pltpu.roll(c, 96, 2), d),
    )
    return a, b, c, d


def build_bands(row_taps, col_taps, a_hi, a_lo, at_hi, at_lo, b_both, bt_both, pad):
    pad[...] = jnp.zeros_like(pad)
    pad[0:8, 0:TAPS] = row_taps[...]
    pad[8:16, 0:TAPS] = col_taps[...]
    c = lax.broadcasted_iota(I32, (256, 256), 0)
    p = lax.broadcasted_iota(I32, (256, 256), 1)
    placed = (c & ~31) + ((c & 3) << 3) + ((c & 31) >> 2)
    permute = (p == placed).astype(F32).astype(BF16)

    def shifted(line):
        row = pad[pl.ds(line, 1), :]
        return pltpu.roll(jnp.broadcast_to(row, (128, 256)), 0, 1, stride=1, stride_axis=0)

    for k in range(KERNELS):
        rows = pl.ds(k * 128, 128)
        for part, a_out, at_out in zip(split(shifted(k)), (a_hi, a_lo), (at_hi, at_lo)):
            ordered = mm(part, permute)
            a_out[rows, :] = ordered.astype(BF16)
            at_out[:, rows] = ordered.T.astype(BF16)
        for i, part in enumerate(split(shifted(8 + k))):
            part = part.astype(F32)
            lanes = pl.ds(i * 128, 128)
            b_both[k, :, lanes] = part.T.astype(BF16)
            bt_both[k, 0:128, lanes] = part[:, 128:256].astype(BF16)
            bt_both[k, 128:256, lanes] = part[:, 0:128].astype(BF16)


def image_gradient(
    weight, wide, target, a_hi, a_lo, at_hi, at_lo, b_both, bt_both, out,
    x_hi, x_lo, y_hi, y_lo, fields, p_hi, p_lo, q_hi, q_lo,
):
    x_hi[192:256, :] = jnp.zeros((64, GROUPS * 128), BF16)
    x_lo[192:256, :] = jnp.zeros((64, GROUPS * 128), BF16)
    for g in range(GROUPS):
        turned = swap_blocks([wide[:, 4 * g + q] for q in range(4)])
        value = jnp.concatenate(turned, axis=1).reshape(192, 128)
        lanes = pl.ds(g * 128, 128)
        x_hi[0:192, lanes], x_lo[0:192, lanes] = split(value)
    for g in range(GROUPS):
        lanes = pl.ds(g * 128, 128)
        high, low = x_hi[:, lanes], x_lo[:, lanes]
        both = mm(a_hi[...], jnp.concatenate([high, low], axis=1))
        value = both[:, :128] + both[:, 128:] + mm(a_lo[...], high)
        y_hi[:, g], y_lo[:, g] = (v.reshape(KERNELS, 128, 128) for v in split(value))
    intensity = jnp.zeros((1024, 128), F32)
    for k in range(KERNELS):
        def window(ref):
            return jnp.concatenate(
                [ref[k, 0:8].reshape(1024, 128), ref[k, 1:9].reshape(1024, 128)], axis=1
            )
        both = mm(window(y_hi), b_both[k])
        field = both[:, :128] + both[:, 128:] + mm(window(y_lo), b_both[k, :, 0:128])
        fields[k] = field
        intensity = intensity + weight[k] * field * field
    wanted = jnp.concatenate([target[:, 128 * n:128 * n + 128] for n in range(8)], axis=0)
    resist = 1.0 / (1.0 + jnp.exp(-STEEPNESS * (intensity - THRESHOLD)))
    sensitivity = 2.0 * (resist - wanted) * STEEPNESS * resist * (1.0 - resist)
    for ref in (p_hi, p_lo):
        ref[0] = jnp.zeros((128, 128), BF16)
        ref[9] = jnp.zeros((128, 128), BF16)
    for k in range(KERNELS):
        product = (2.0 * weight[k]) * sensitivity * fields[k]
        p_hi[1:9], p_lo[1:9] = (v.reshape(8, 128, 128) for v in split(product))

        def window(ref):
            return jnp.concatenate(
                [ref[0:9].reshape(1152, 128), ref[1:10].reshape(1152, 128)], axis=1
            )
        both = mm(window(p_hi), bt_both[k])
        value = both[:, :128] + both[:, 128:] + mm(window(p_lo), bt_both[k, :, 0:128])
        high, low = split(value)
        for g in range(GROUPS):
            lanes = pl.ds(g * 128, 128)
            rows = pl.ds(k * 128, 128)
            q_hi[rows, lanes] = high[128 * g:128 * g + 128]
            q_lo[rows, lanes] = low[128 * g:128 * g + 128]
    for g in range(GROUPS):
        lanes = pl.ds(g * 128, 128)
        high, low = q_hi[:, lanes], q_lo[:, lanes]
        both = mm(at_hi[0:192, :], jnp.concatenate([high, low], axis=1))
        value = both[:, :128] + both[:, 128:] + mm(at_lo[0:192, :], high)
        value = value.reshape(6, 32, 128)
        turned = swap_blocks([value[:, 8 * s:8 * s + 8] for s in range(4)])
        for q in range(4):
            out[:, 4 * g + q] = turned[q]


def exists(at, counts, step):
    ok = None
    for a, count, d in zip(at, counts, step):
        if d:
            here = (a + d >= 0) if d < 0 else (a + d < count)
            ok = here if ok is None else jnp.logical_and(ok, here)
    return ok


def exchange(copy, at, counts):
    for i, (dr, dc) in enumerate(NEIGHBOURS):
        @pl.when(exists(at, counts, (dr, dc)))
        def _():
            copy(i, dr, dc).start()
    for i, (dr, dc) in enumerate(NEIGHBOURS):
        @pl.when(exists(at, counts, (dr, dc)))
        def _():
            copy(i, dr, dc).wait_send()

        @pl.when(exists(at, counts, (-dr, -dc)))
        def _():
            copy(i, dr, dc).wait_recv()


def hops(step):
    return sum(min(d, 4 - d) for d in step[:3])


STEPS = sorted((s for s in itertools.product(range(4), range(4), range(4), range(2)) if any(s)), key=lambda s: -hops(s))


def step_kernel(
    counts, weight, inst, cells, row_taps, col_taps, target, out,
    pad, mine, table, cells3, outgoing, arrived, index_v, index_s, where_v, where_s, tile_v, tile_s, wide,
    a_hi, a_lo, at_hi, at_lo, b_both, bt_both, taps_pad,
    x_hi, x_lo, y_hi, y_lo, fields, p_hi, p_lo, q_hi, q_lo,
    grad, halo_row, halo_col, halo_corner, own, back,
    table_send, table_recv, block_send, block_recv, cell_send, cell_recv, grad_send, grad_recv,
    halo_send, halo_recv, rim_send, rim_recv, local,
):
    row_count, col_count = counts
    total = row_count * col_count
    at = row, col = lax.axis_index("row"), lax.axis_index("col")
    me = row * col_count + col
    barrier = pltpu.get_barrier_semaphore()
    row_peers = [(row, lax.rem(col + i, col_count)) for i in range(1, col_count)]
    col_peers = [(lax.rem(row + i, row_count), col) for i in range(1, row_count)]

    def remote(source, target, send, recv, where):
        return pltpu.make_async_remote_copy(
            src_ref=source, dst_ref=target, send_sem=send, recv_sem=recv,
            device_id=where, device_id_type=MESH,
        )

    for a in (0, 5):
        wide[a] = jnp.zeros((WIDE, 8, 128), F32)
    for b in (0, 33, 34, 35):
        wide[1:5, b] = jnp.zeros((TILE_ROWS, 8, 128), F32)
    for ref in (halo_row, halo_col, halo_corner):
        ref[...] = jnp.zeros_like(ref)
    for where in row_peers + col_peers:
        pl.semaphore_signal(barrier, inc=1, device_id=where, device_id_type=MESH)
    pad[...] = jnp.zeros_like(pad)
    pad[0:TILE_ROWS, 0:TILE_COLS] = inst[...]
    lines = pad[...]
    line = lax.broadcasted_iota(I32, lines.shape, 0)
    flat = jnp.zeros((8, 128), I32)
    for a in range(TILE_ROWS):
        moved = pltpu.roll(lines, 32 * a, 1) if a else lines
        flat = flat + jnp.where(line == a, moved, 0)
    flat = jnp.sum(flat, axis=0, keepdims=True)
    mine[0] = flat
    table[me] = flat
    for r in range(8):
        cells3[:, r, :] = cells[:, 128 * r:128 * r + 128]
    pl.semaphore_wait(barrier, len(row_peers) + len(col_peers))

    for where in row_peers:
        remote(mine, table.at[pl.ds(me, 1)], table_send, table_recv, where).start()
    lane = lax.broadcasted_iota(I32, (128, 128), 1)
    sub = lax.broadcasted_iota(I32, (128, 128), 0)
    diagonal = lane == sub

    def as_row(column):
        return jnp.sum(jnp.where(diagonal, column, 0), axis=0, keepdims=True)
    owner = flat >> 5
    held = owner == sub
    first = jnp.min(jnp.where(held, lane, TILES), axis=1, keepdims=True)
    last = jnp.max(jnp.where(held, lane, -1), axis=1, keepdims=True)
    second = jnp.sum(jnp.where(held & (lane != first), 1, 0), axis=0, keepdims=True)
    tile_v[0:1, :] = as_row(jnp.minimum(first, TILES - 1))
    tile_v[1:2, :] = as_row(jnp.maximum(last, 0))
    where_v[...] = owner * 2 + second
    where_copy = pltpu.make_async_copy(where_v, where_s, local.at[0])
    tile_copy = pltpu.make_async_copy(tile_v, tile_s, local.at[1])
    where_copy.start()
    tile_copy.start()
    others = table.at[pl.ds(0, len(row_peers))]
    remote(others, others, table_send, table_recv, row_peers[0]).wait()
    block = table.at[pl.ds(row * col_count, col_count)]
    for where in col_peers:
        remote(block, block, block_send, block_recv, where).start()
    others = table.at[pl.ds(0, len(col_peers) * col_count)]
    remote(others, others, block_send, block_recv, col_peers[0]).wait()

    asked = table[...].reshape(128, 128)
    hit = (asked >> 5) == me
    key = lane * SLOTS + (asked & (SLOTS - 1))
    first = jnp.min(jnp.where(hit, key, TILES * SLOTS), axis=1, keepdims=True)
    last = jnp.max(jnp.where(hit, key, -1), axis=1, keepdims=True)
    chosen = (
        as_row(jnp.where(first < TILES * SLOTS, first & (SLOTS - 1), -1)),
        as_row(jnp.where(last > first, last & (SLOTS - 1), -1)),
    )
    for s in range(2):
        index_v[s:s + 1, :] = jnp.maximum(chosen[s], 0)
    cell = lax.broadcasted_iota(I32, (SLOTS, 128), 0)
    selector = jnp.concatenate([(cell == c).astype(F32).astype(BF16) for c in chosen], axis=1)
    index_copy = pltpu.make_async_copy(index_v, index_s, local.at[2])
    index_copy.start()

    core, z = lax.rem(row, 2), lax.rem(row // 2, 4)
    y, x = (row // 8) * 2 + lax.rem(col, 2), col // 2

    def everyone(source, index, landing, send, recv):
        for dx, dy, dz, dcore in STEPS:
            to_y = lax.rem(y + dy, 4)
            to_row = (to_y // 2) * 8 + lax.rem(z + dz, 4) * 2 + lax.rem(core + dcore, 2)
            to_col = lax.rem(x + dx, 4) * 2 + lax.rem(to_y, 2)
            peer = to_row * col_count + to_col
            for s in range(2):
                outgoing[2 * peer + s] = source[index[s, peer]]
            remote(
                outgoing.at[pl.ds(2 * peer, 2)], landing.at[pl.ds(2 * me, 2)], send, recv, (to_row, to_col)
            ).start()
        for s in range(2):
            landing[2 * me + s] = source[index[s, me]]

    def everyone_wait(landing, send, recv):
        others = pl.ds(0, 2 * (total - 1))
        remote(outgoing.at[others], landing.at[others], send, recv, row_peers[0]).wait()

    index_copy.wait()
    everyone(cells3, index_s, arrived, cell_send, cell_recv)
    where_copy.wait()
    tile_copy.wait()
    build_bands(row_taps, col_taps, a_hi, a_lo, at_hi, at_lo, b_both, bt_both, taps_pad)
    everyone_wait(arrived, cell_send, cell_recv)

    def put(t, carry):
        wide[1 + t // TILE_COLS, 1 + lax.rem(t, TILE_COLS)] = arrived[where_s[0, t]]
        return carry
    lax.fori_loop(0, TILES, put, 0, unroll=8)

    def halo(i, dr, dc):
        return remote(
            wide.at[span(dr, TILE_ROWS, True), span(dc, TILE_COLS, True)],
            wide.at[span(-dr, TILE_ROWS, False), span(-dc, TILE_COLS, False)],
            halo_send.at[i], halo_recv.at[i], (row + dr, col + dc),
        )
    exchange(halo, at, counts)

    image_gradient(
        weight, wide, target, a_hi, a_lo, at_hi, at_lo, b_both, bt_both, grad,
        x_hi, x_lo, y_hi, y_lo, fields, p_hi, p_lo, q_hi, q_lo,
    )

    def rim(i, dr, dc):
        side_row, side_col = 0 if dr < 0 else TILE_ROWS + 1, 0 if dc < 0 else TILE_COLS + 1
        if dr == 0:
            source, landing = grad.at[pl.ds(1, TILE_ROWS), side_col], halo_col.at[0 if dc < 0 else 1]
        elif dc == 0:
            source, landing = grad.at[side_row, pl.ds(1, TILE_COLS)], halo_row.at[0 if dr < 0 else 1]
        else:
            source, landing = grad.at[side_row, side_col], halo_corner.at[2 * (dr > 0) + (dc > 0)]
        return remote(source, landing, rim_send.at[i], rim_recv.at[i], (row + dr, col + dc))
    exchange(rim, at, counts)
    own[...] = grad[1:5, 1:33].reshape(TILES, 8, 128)
    own[96:128] = own[96:128] + halo_row[0]
    own[0:32] = own[0:32] + halo_row[1]
    for a in range(TILE_ROWS):
        t = TILE_COLS * a
        own[t + 31] = own[t + 31] + halo_col[0, a]
        own[t] = own[t] + halo_col[1, a]
    for i, t in enumerate((127, 96, 31, 0)):
        own[t] = own[t] + halo_corner[i]

    everyone(own, tile_s, back, grad_send, grad_recv)
    everyone_wait(back, grad_send, grad_recv)
    flat = back.reshape(2 * TILES * 8, 128)
    for r in range(8):
        value = jnp.concatenate(
            [flat[pl.ds(8 * s + r, 128, stride=16), :] for s in range(2)], axis=0
        )
        high, low = split(value)
        tail = (value - high.astype(F32) - low.astype(F32)).astype(BF16)
        parts = mm(selector, jnp.concatenate([high, low, tail], axis=1))
        total_r = parts[:, 0:128] + parts[:, 128:256] + parts[:, 256:384]
        lanes = slice(128 * r, 128 * r + 128)
        out[:, lanes] = cells[:, lanes] - STEP_RATE * total_r


def shards(counts, cells, instance_cell, target, row_taps, col_taps, kernel_weight):
    vmem = pltpu.VMEM
    smem = pltpu.SMEM
    dma = pltpu.SemaphoreType.DMA
    return pl.pallas_call(
        functools.partial(step_kernel, counts),
        name="gradient_step",
        out_shape=jax.ShapeDtypeStruct((SLOTS, 1024), F32),
        in_specs=[SCALARS] + [WHOLE] * 5,
        out_specs=WHOLE,
        scratch_shapes=[
            vmem((8, 128), I32), vmem((1, 1, 128), I32), vmem((128, 1, 128), I32),
            vmem((SLOTS, 8, 128), F32), vmem((256, 8, 128), F32), vmem((256, 8, 128), F32),
            vmem((2, 128), I32), smem((2, 128), I32), vmem((1, 128), I32), smem((1, 128), I32),
            vmem((2, 128), I32), smem((2, 128), I32), vmem((6, WIDE, 8, 128), F32),
            vmem((1024, 256), BF16), vmem((1024, 256), BF16), vmem((256, 1024), BF16), vmem((256, 1024), BF16),
            vmem((8, 256, 256), BF16), vmem((8, 256, 256), BF16), vmem((16, 256), F32),
            vmem((256, 1152), BF16), vmem((256, 1152), BF16),
            vmem((8, 9, 128, 128), BF16), vmem((8, 9, 128, 128), BF16),
            vmem((8, 1024, 128), F32),
            vmem((10, 128, 128), BF16), vmem((10, 128, 128), BF16),
            vmem((1024, 1152), BF16), vmem((1024, 1152), BF16),
            vmem((6, WIDE, 8, 128), F32),
            vmem((2, 32, 8, 128), F32), vmem((2, 4, 8, 128), F32), vmem((4, 8, 128), F32),
            vmem((TILES, 8, 128), F32), vmem((256, 8, 128), F32),
        ] + [dma] * 8 + [dma((8,))] * 4 + [dma((3,))],
        compiler_params=pltpu.CompilerParams(collective_id=0, has_side_effects=True),
    )(kernel_weight, instance_cell, cells, row_taps, col_taps, target)


def solution(mesh):
    placed = (P(("row", "col"), None), P("row", "col"), P("row", "col"), P(), P(), P())
    return jax.shard_map(
        functools.partial(shards, (mesh.shape["row"], mesh.shape["col"])),
        mesh=mesh, in_specs=placed, out_specs=P(("row", "col"), None), check_vma=False,
    )
```

time: 94.7 us -> 72.9 us (0.77)
  Pallas kernels: 92.9 us -> 71.2 us
    pallas_call x4 -> x1, Pallas kernels: 92.9 us -> 71.2 us  [shards(): pl.pallas_call(functools.partial(step_kernel, counts), name='gradient_ste...]
where the time goes in v1:
time: 72.9 us; the launch traced here: 72.7 us
  Pallas kernels  71.2 us (98%)
  local copies, waits for them, and re-layouts  1.57 us (2%)
    pallas_call x1, Pallas kernels, shards(): pl.pallas_call(functools.partial(step_kernel, counts), name='gradient_ste...  71.2 us
    unnamed x1, local copies, waits for them, and re-layouts  1.57 us

profile of v1, /device:TPU:1, one launch (start us, length us, event | category | flops | bytes accessed | tf_op | source)
XLA Modules:
  0.0 72.7 jit_solution(17509954691232563700)
XLA Ops:
  0.0 71.2 %gradient_step.1 = f32[32,1024]{1,0:T(8,128)} custom-call(f32[8]{0:T(128)} %weight.1, s32[4,32]{1,0:T(4,128)} %inst.1, f32[32,1024]{1,0:T(8,128)} %cells.1, f32[8,65]{1,0:T(8,128)} %row_taps.1, f32[8,65]{1,0:T(8,128)} %col_taps.1, f32[128,1024]{1,0:T(8,128)} %target.1), custom_call_target="tpu_custom_call" | custom-call | tf_op jit(solution)/shard_map/gradient_step/pallas_call | solution.py:369
  71.2 1.6 %copy.8 = f32[32,1024]{1,0:T(8,128)} copy(f32[32,1024]{1,0:T(8,128)} %gradient_step.1) | data formatting | bytes 262144

commit v2 on v1

v2 whole, which is shorter than its diff:
```python
import functools
import itertools

import jax
import jax.numpy as jnp
from jax import lax
from jax.experimental import pallas as pl
from jax.experimental.pallas import tpu as pltpu
from jax.sharding import PartitionSpec as P

TILE = 32
TAPS = 65
KERNELS = 8
ROWS = 128
COLS = 1024
TILE_ROWS = 4
TILE_COLS = 32
TILES = 128
SLOTS = 32
WIDE = 36
GROUPS = 9
STEEPNESS = 4.0
THRESHOLD = 0.3
STEP_RATE = 0.5
MESH = pl.DeviceIdType.MESH
BF16 = jnp.bfloat16
F32 = jnp.float32
I32 = jnp.int32
WHOLE = pl.BlockSpec(memory_space=pltpu.VMEM)
SCALARS = pl.BlockSpec(memory_space=pltpu.SMEM)

NEIGHBOURS = tuple((dr, dc) for dr in (-1, 0, 1) for dc in (-1, 0, 1) if (dr, dc) != (0, 0))


def span(step, count, inside):
    if step == 0:
        return pl.ds(1, count)
    if step < 0:
        return pl.ds(1 if inside else 0, 1)
    return pl.ds(count if inside else count + 1, 1)


def split(value):
    high = value.astype(BF16)
    return high, (value - high.astype(F32)).astype(BF16)


def mm(a, b):
    return jnp.dot(a, b, preferred_element_type=F32)


def swap_blocks(vectors):
    lane = lax.broadcasted_iota(I32, vectors[0].shape, 2)
    low = lane < 64
    even = (lane & 32) == 0
    a, b, c, d = vectors
    a, c = (
        jnp.where(low, a, pltpu.roll(c, 64, 2)),
        jnp.where(low, pltpu.roll(a, 64, 2), c),
    )
    b, d = (
        jnp.where(low, b, pltpu.roll(d, 64, 2)),
        jnp.where(low, pltpu.roll(b, 64, 2), d),
    )
    a, b = (
        jnp.where(even, a, pltpu.roll(b, 32, 2)),
        jnp.where(even, pltpu.roll(a, 96, 2), b),
    )
    c, d = (
        jnp.where(even, c, pltpu.roll(d, 32, 2)),
        jnp.where(even, pltpu.roll(c, 96, 2), d),
    )
    return a, b, c, d


def build_bands(row_taps, col_taps, a_own, a_halo, at_own, at_halo, b_both, bt_both, pad):
    pad[...] = jnp.zeros_like(pad)
    pad[0:8, 0:TAPS] = row_taps[...]
    pad[8:16, 0:TAPS] = col_taps[...]
    c = lax.broadcasted_iota(I32, (256, 256), 0)
    p = lax.broadcasted_iota(I32, (256, 256), 1)
    inner = ((c & 3) << 3) + ((c & 31) >> 2)
    tile = c >> 5
    is_own = (tile >= 1) & (tile <= 4)
    own_at = jnp.where(is_own, 32 * tile - 32 + inner, -1024)
    halo_at = jnp.where(tile == 0, inner, jnp.where(tile == 5, 32 + inner, -1024))

    def ones(condition):
        return condition.astype(F32).astype(BF16)
    own_high, own_low = ones(p == own_at), ones(p == own_at + 128)
    halo_high, halo_low = ones((p == halo_at) | (p == halo_at + 128)), ones(p == halo_at + 64)

    def shifted(line):
        row = pad[pl.ds(line, 1), :]
        return pltpu.roll(jnp.broadcast_to(row, (128, 256)), 0, 1, stride=1, stride_axis=0)

    for k in range(KERNELS):
        rows = pl.ds(k * 128, 128)
        high, low = split(shifted(k))
        own = mm(high, own_high) + mm(low, own_low)
        halo = mm(high, halo_high) + mm(low, halo_low)
        a_own[rows, :] = own.astype(BF16)
        a_halo[rows, :] = halo.astype(BF16)
        at_own[:, rows] = own.T.astype(BF16)
        at_halo[:, rows] = halo.T[0:128].astype(BF16)
        for i, part in enumerate(split(shifted(8 + k))):
            part = part.astype(F32)
            lanes = pl.ds(i * 128, 128)
            b_both[k, :, lanes] = part.T.astype(BF16)
            bt_both[k, 0:128, lanes] = part[:, 128:256].astype(BF16)
            bt_both[k, 128:256, lanes] = part[:, 0:128].astype(BF16)


def lanes_of(g, count=1):
    return pl.ds(g * 128, 128 * count)


EARLY = (1, 3, 5)


def mask_own(g, wide, x_own, x_low):
    turned = swap_blocks([wide[1:5, 4 * g + q] for q in range(4)])
    high, low = split(jnp.concatenate(turned, axis=1).reshape(128, 128))
    x_own[0:128, lanes_of(g)] = high
    x_own[128:256, lanes_of(g)] = high
    x_low[:, lanes_of(g)] = low


def rows_own(wide, a_own, x_own, x_low, early):
    for i, g in enumerate(EARLY):
        for h in (g, g + 1):
            mask_own(h, wide, x_own, x_low)
        lanes = lanes_of(g, 2)
        early[i] = mm(a_own[...], x_own[:, lanes]) + mm(a_own[:, 0:128], x_low[:, lanes])
    mask_own(7, wide, x_own, x_low)


def forward(weight, wide, a_own, a_halo, b_both, x_own, x_low, x_halo, early, y_hi, y_lo, fields, power):
    for g in (0, 8):
        mask_own(g, wide, x_own, x_low)
    x_halo[192:256, :] = jnp.zeros((64, GROUPS * 128), BF16)
    for g in range(GROUPS):
        sides = [jnp.stack([wide[0, 4 * g + q], wide[5, 4 * g + q]]) for q in range(4)]
        value = jnp.concatenate(swap_blocks(sides), axis=1).reshape(64, 128)
        high, low = split(value)
        lanes = lanes_of(g)
        x_halo[0:64, lanes] = high
        x_halo[64:128, lanes] = high
        x_halo[128:192, lanes] = low

    def keep(g, value):
        y_hi[:, g], y_lo[:, g] = (v.reshape(KERNELS, 128, 128) for v in split(value))
    lanes = lanes_of(7, 2)
    value = (
        mm(a_own[...], x_own[:, lanes]) + mm(a_own[:, 0:128], x_low[:, lanes]) + mm(a_halo[...], x_halo[:, lanes])
    )
    for h in range(2):
        keep(7 + h, value[:, 128 * h:128 * h + 128])
    lanes = lanes_of(0)
    beside = jnp.concatenate([x_low[:, lanes], jnp.zeros((128, 128), BF16)], axis=0)
    both = mm(a_own[...], jnp.concatenate([x_own[:, lanes], beside], axis=1))
    keep(0, both[:, 0:128] + both[:, 128:256] + mm(a_halo[...], x_halo[:, lanes]))
    for i, g in enumerate(EARLY):
        value = early[i] + mm(a_halo[...], x_halo[:, lanes_of(g, 2)])
        for h in range(2):
            keep(g + h, value[:, 128 * h:128 * h + 128])
    for k in range(KERNELS):
        def window(ref):
            return jnp.concatenate(
                [ref[k, 0:8].reshape(1024, 128), ref[k, 1:9].reshape(1024, 128)], axis=1
            )
        both = mm(window(y_hi), b_both[k])
        field = both[:, :128] + both[:, 128:] + mm(window(y_lo), b_both[k, :, 0:128])
        fields[k] = field
        share = weight[k] * field * field
        power[...] = share if k == 0 else power[...] + share


def adjoint_columns(weight, target, bt_both, fields, power, p_hi, p_lo, q_hi, q_lo):
    for n in range(8):
        part = pl.ds(128 * n, 128)
        wanted = target[:, part]
        resist = 1.0 / (1.0 + jnp.exp(-STEEPNESS * (power[part, :] - THRESHOLD)))
        power[part, :] = (2.0 * STEEPNESS * 2.0) * (resist - wanted) * resist * (1.0 - resist)
    for k in range(KERNELS):
        high, low = p_hi.at[k % 2], p_lo.at[k % 2]
        product = weight[k] * power[...] * fields[k]
        high[1:9], low[1:9] = (v.reshape(8, 128, 128) for v in split(product))

        def window(ref):
            return jnp.concatenate(
                [ref[0:9].reshape(1152, 128), ref[1:10].reshape(1152, 128)], axis=1
            )
        both = mm(window(high), bt_both[k])
        value = both[:, :128] + both[:, 128:] + mm(window(low), bt_both[k, :, 0:128])
        high, low = split(value)
        for g in range(GROUPS):
            rows = pl.ds(k * 128, 128)
            q_hi[rows, lanes_of(g)] = high[128 * g:128 * g + 128]
            q_lo[rows, lanes_of(g)] = low[128 * g:128 * g + 128]


def adjoint_rows(bands, count, g, q_hi, q_lo):
    tiles = []
    if g == GROUPS - 1:
        lanes = lanes_of(g)
        both = mm(bands[...], jnp.concatenate([q_hi[:, lanes], q_lo[:, lanes]], axis=1))
        both = both[:, 0:128] + both[:, 128:256]
        parts = [both[0:count] + both[count:2 * count]]
    else:
        lanes = lanes_of(g, 2)
        both = mm(bands[...], q_hi[:, lanes])
        value = both[0:count] + both[count:2 * count] + mm(bands[0:count, :], q_lo[:, lanes])
        parts = [value[:, 0:128], value[:, 128:256]]
    for h, value in enumerate(parts):
        value = value.reshape(count // 32, 32, 128)
        turned = swap_blocks([value[:, 8 * s:8 * s + 8] for s in range(4)])
        tiles += [(4 * (g + h) + q, turned[q]) for q in range(4)]
    return tiles


def exists(at, counts, step):
    ok = None
    for a, count, d in zip(at, counts, step):
        if d:
            here = (a + d >= 0) if d < 0 else (a + d < count)
            ok = here if ok is None else jnp.logical_and(ok, here)
    return ok


def start_copies(copy, at, counts, which):
    for i in which:
        @pl.when(exists(at, counts, NEIGHBOURS[i]))
        def _():
            copy(i, *NEIGHBOURS[i]).start()


def wait_copies(copy, at, counts):
    for i, (dr, dc) in enumerate(NEIGHBOURS):
        @pl.when(exists(at, counts, (dr, dc)))
        def _():
            copy(i, dr, dc).wait_send()

        @pl.when(exists(at, counts, (-dr, -dc)))
        def _():
            copy(i, dr, dc).wait_recv()


ACROSS = sorted((i for i, (dr, dc) in enumerate(NEIGHBOURS) if dr), key=lambda i: NEIGHBOURS[i][1] == 0)
ALONG = [i for i, (dr, dc) in enumerate(NEIGHBOURS) if not dr]


def hops(step):
    return sum(min(d, 4 - d) for d in step[:3])


STEPS = sorted((s for s in itertools.product(range(4), range(4), range(4), range(2)) if any(s)), key=lambda s: -hops(s))


def step_kernel(
    counts, weight, inst, cells, row_taps, col_taps, target_hbm, out,
    pad, table, cells3, outgoing, arrived, index_v, index_s, where_v, where_s, tile_v, tile_s, wide, target,
    a_own, a_halo, at_own, at_halo, b_both, bt_both, taps_pad,
    x_own, x_low, x_halo, early, y_hi, y_lo, fields, power, p_hi, p_lo, q_hi, q_lo,
    rim_row, rim_col, halo_row, halo_col, halo_corner, own, back,
    table_send, table_recv, block_send, block_recv, cell_send, cell_recv, grad_send, grad_recv,
    halo_send, halo_recv, rim_send, rim_recv, local,
):
    row_count, col_count = counts
    total = row_count * col_count
    at = row, col = lax.axis_index("row"), lax.axis_index("col")
    me = row * col_count + col
    barrier = pltpu.get_barrier_semaphore()
    core, z = lax.rem(row, 2), lax.rem(row // 2, 4)
    y, x = (row // 8) * 2 + lax.rem(col, 2), col // 2

    def device(step):
        dx, dy, dz, dcore = step
        to = lax.rem(x + dx, 4), lax.rem(y + dy, 4), lax.rem(z + dz, 4), lax.rem(core + dcore, 2)
        where = (to[1] // 2) * 8 + to[2] * 2 + to[3], to[0] * 2 + lax.rem(to[1], 2)
        return where, ((to[0] * 4 + to[1]) * 4 + to[2]) * 2 + to[3]
    rank = ((x * 4 + y) * 4 + z) * 2 + core
    near = [device(s)[0] for s in STEPS if s[0] == s[1] == 0]
    far = [device(s)[0] for s in STEPS if s[2] == s[3] == 0]

    def remote(source, landing, send, recv, where):
        return pltpu.make_async_remote_copy(
            src_ref=source, dst_ref=landing, send_sem=send, recv_sem=recv,
            device_id=where, device_id_type=MESH,
        )

    for a in (0, 5):
        wide[a] = jnp.zeros((WIDE, 8, 128), F32)
    for b in (0, 33, 34, 35):
        wide[1:5, b] = jnp.zeros((TILE_ROWS, 8, 128), F32)
    for ref in (halo_row, halo_col, halo_corner):
        ref[...] = jnp.zeros_like(ref)
    for where in far + near:
        pl.semaphore_signal(barrier, inc=1, device_id=where, device_id_type=MESH)
    target_copy = pltpu.make_async_copy(target_hbm, target, local.at[3])
    target_copy.start()
    pad[...] = jnp.zeros_like(pad)
    pad[0:TILE_ROWS, 0:TILE_COLS] = inst[...]
    lines = pad[...]
    line = lax.broadcasted_iota(I32, lines.shape, 0)
    flat = jnp.zeros((8, 128), I32)
    for a in range(TILE_ROWS):
        moved = pltpu.roll(lines, 32 * a, 1) if a else lines
        flat = flat + jnp.where(line == a, moved, 0)
    flat = jnp.sum(flat, axis=0, keepdims=True)
    table[rank] = flat
    for r in range(8):
        cells3[:, r, :] = cells[:, 128 * r:128 * r + 128]
    lane = lax.broadcasted_iota(I32, (128, 128), 1)
    sub = lax.broadcasted_iota(I32, (128, 128), 0)
    diagonal = lane == sub

    def as_row(column):
        return jnp.sum(jnp.where(diagonal, column, 0), axis=0, keepdims=True)
    owner = flat >> 5
    held = owner == sub
    first = jnp.min(jnp.where(held, lane, TILES), axis=1, keepdims=True)
    last = jnp.max(jnp.where(held, lane, -1), axis=1, keepdims=True)
    second = jnp.sum(jnp.where(held & (lane != first), 1, 0), axis=0, keepdims=True)
    tile_v[0:1, :] = as_row(jnp.minimum(first, TILES - 1))
    tile_v[1:2, :] = as_row(jnp.maximum(last, 0))
    where_v[...] = owner * 2 + second
    where_copy = pltpu.make_async_copy(where_v, where_s, local.at[0])
    tile_copy = pltpu.make_async_copy(tile_v, tile_s, local.at[1])
    where_copy.start()
    tile_copy.start()
    pl.semaphore_wait(barrier, len(near) + len(far))

    mine = table.at[pl.ds(rank, 1)]
    for where in near:
        remote(mine, mine, table_send, table_recv, where).start()
    others = table.at[pl.ds(0, len(near))]
    remote(others, others, table_send, table_recv, near[0]).wait()
    block = table.at[pl.ds((x * 4 + y) * 8, 8)]
    for where in far:
        remote(block, block, block_send, block_recv, where).start()
    others = table.at[pl.ds(0, len(far) * 8)]
    remote(others, others, block_send, block_recv, far[0]).wait()

    asked = table[...].reshape(128, 128)
    hit = (asked >> 5) == me
    key = lane * SLOTS + (asked & (SLOTS - 1))
    first = jnp.min(jnp.where(hit, key, TILES * SLOTS), axis=1, keepdims=True)
    last = jnp.max(jnp.where(hit, key, -1), axis=1, keepdims=True)
    chosen = (
        as_row(jnp.where(first < TILES * SLOTS, first & (SLOTS - 1), -1)),
        as_row(jnp.where(last > first, last & (SLOTS - 1), -1)),
    )
    for s in range(2):
        index_v[s:s + 1, :] = jnp.maximum(chosen[s], 0)
    cell = lax.broadcasted_iota(I32, (SLOTS, 128), 0)
    selector = jnp.concatenate([(cell == c).astype(F32).astype(BF16) for c in chosen], axis=1)
    index_copy = pltpu.make_async_copy(index_v, index_s, local.at[2])
    index_copy.start()

    def everyone(source, index, by_rank, landing, place, send, recv):
        for i, step in enumerate(STEPS):
            where, to_rank = device(step)
            peer = to_rank if by_rank else where[0] * col_count + where[1]
            for s in range(2):
                outgoing[2 * i + s] = source[index[s, peer]]
            remote(
                outgoing.at[pl.ds(2 * i, 2)], landing.at[pl.ds(2 * place, 2)], send, recv, where
            ).start()
        for s in range(2):
            landing[2 * place + s] = source[index[s, rank if by_rank else me]]

    def everyone_wait(landing, send, recv):
        others = pl.ds(0, 2 * (total - 1))
        remote(outgoing.at[others], landing.at[others], send, recv, near[0]).wait()

    index_copy.wait()
    everyone(cells3, index_s, True, arrived, me, cell_send, cell_recv)
    where_copy.wait()
    tile_copy.wait()
    target_copy.wait()
    build_bands(row_taps, col_taps, a_own, a_halo, at_own, at_halo, b_both, bt_both, taps_pad)
    for ref in (p_hi, p_lo):
        for parity in range(2):
            ref[parity, 0] = jnp.zeros((128, 128), BF16)
            ref[parity, 9] = jnp.zeros((128, 128), BF16)
    everyone_wait(arrived, cell_send, cell_recv)

    def put(t, carry):
        wide[1 + t // TILE_COLS, 1 + lax.rem(t, TILE_COLS)] = arrived[where_s[0, t]]
        return carry
    lax.fori_loop(0, TILES, put, 0, unroll=8)

    def halo(i, dr, dc):
        return remote(
            wide.at[span(dr, TILE_ROWS, True), span(dc, TILE_COLS, True)],
            wide.at[span(-dr, TILE_ROWS, False), span(-dc, TILE_COLS, False)],
            halo_send.at[i], halo_recv.at[i], (row + dr, col + dc),
        )
    start_copies(halo, at, counts, ACROSS + ALONG)
    rows_own(wide, a_own, x_own, x_low, early)
    wait_copies(halo, at, counts)

    forward(weight, wide, a_own, a_halo, b_both, x_own, x_low, x_halo, early, y_hi, y_lo, fields, power)
    adjoint_columns(weight, target, bt_both, fields, power, p_hi, p_lo, q_hi, q_lo)

    def rim(i, dr, dc):
        side_row, side_col = int(dr > 0), 0 if dc < 0 else TILE_COLS + 1
        if dr == 0:
            source, landing = rim_col.at[int(dc > 0)], halo_col.at[int(dc > 0)]
        elif dc == 0:
            source, landing = rim_row.at[side_row, pl.ds(1, TILE_COLS)], halo_row.at[side_row]
        else:
            source, landing = rim_row.at[side_row, side_col], halo_corner.at[2 * side_row + int(dc > 0)]
        return remote(source, landing, rim_send.at[i], rim_recv.at[i], (row + dr, col + dc))

    for g in (0, 2, 4, 6, 8):
        for c, tiles in adjoint_rows(at_halo, 64, g, q_hi, q_lo):
            rim_row[:, c] = tiles
    start_copies(rim, at, counts, ACROSS)
    for g in (0, 8, 2, 4, 6):
        for c, tiles in adjoint_rows(at_own, 128, g, q_hi, q_lo):
            if c in (0, TILE_COLS + 1):
                rim_col[int(c > 0)] = tiles
            elif c <= TILE_COLS:
                for a in range(TILE_ROWS):
                    own[TILE_COLS * a + c - 1] = tiles[a]
        if g == 8:
            start_copies(rim, at, counts, ALONG)
    wait_copies(rim, at, counts)
    own[96:128] = own[96:128] + halo_row[0]
    own[0:32] = own[0:32] + halo_row[1]
    for a in range(TILE_ROWS):
        t = TILE_COLS * a
        own[t + 31] = own[t + 31] + halo_col[0, a]
        own[t] = own[t] + halo_col[1, a]
    for i, t in enumerate((127, 96, 31, 0)):
        own[t] = own[t] + halo_corner[i]

    everyone(own, tile_s, False, back, rank, grad_send, grad_recv)
    everyone_wait(back, grad_send, grad_recv)
    flat = back.reshape(2 * TILES * 8, 128)
    for r in range(8):
        value = jnp.concatenate(
            [flat[pl.ds(8 * s + r, 128, stride=16), :] for s in range(2)], axis=0
        )
        high, low = split(value)
        tail = (value - high.astype(F32) - low.astype(F32)).astype(BF16)
        parts = mm(selector, jnp.concatenate([high, low, tail], axis=1))
        total_r = parts[:, 0:128] + parts[:, 128:256] + parts[:, 256:384]
        lanes = slice(128 * r, 128 * r + 128)
        out[:, lanes] = cells[:, lanes] - STEP_RATE * total_r


def shards(counts, cells, instance_cell, target, row_taps, col_taps, kernel_weight):
    vmem = pltpu.VMEM
    smem = pltpu.SMEM
    dma = pltpu.SemaphoreType.DMA
    return pl.pallas_call(
        functools.partial(step_kernel, counts),
        name="gradient_step",
        out_shape=jax.ShapeDtypeStruct((SLOTS, 1024), F32),
        in_specs=[SCALARS] + [WHOLE] * 4 + [pl.BlockSpec(memory_space=pl.ANY)],
        out_specs=WHOLE,
        scratch_shapes=[
            vmem((8, 128), I32), vmem((128, 1, 128), I32),
            vmem((SLOTS, 8, 128), F32), vmem((256, 8, 128), F32), vmem((256, 8, 128), F32),
            vmem((2, 128), I32), smem((2, 128), I32), vmem((1, 128), I32), smem((1, 128), I32),
            vmem((2, 128), I32), smem((2, 128), I32), vmem((6, WIDE, 8, 128), F32), vmem((ROWS, COLS), F32),
            vmem((1024, 256), BF16), vmem((1024, 256), BF16), vmem((256, 1024), BF16), vmem((128, 1024), BF16),
            vmem((8, 256, 256), BF16), vmem((8, 256, 256), BF16), vmem((16, 256), F32),
            vmem((256, 1152), BF16), vmem((128, 1152), BF16), vmem((256, 1152), BF16),
            vmem((3, 1024, 256), F32),
            vmem((8, 9, 128, 128), BF16), vmem((8, 9, 128, 128), BF16),
            vmem((8, 1024, 128), F32), vmem((1024, 128), F32),
            vmem((2, 10, 128, 128), BF16), vmem((2, 10, 128, 128), BF16),
            vmem((1024, 1152), BF16), vmem((1024, 1152), BF16),
            vmem((2, WIDE, 8, 128), F32), vmem((2, 4, 8, 128), F32),
            vmem((2, 32, 8, 128), F32), vmem((2, 4, 8, 128), F32), vmem((4, 8, 128), F32),
            vmem((TILES, 8, 128), F32), vmem((256, 8, 128), F32),
        ] + [dma] * 8 + [dma((8,))] * 4 + [dma((4,))],
        compiler_params=pltpu.CompilerParams(collective_id=0, has_side_effects=True),
    )(kernel_weight, instance_cell, cells, row_taps, col_taps, target)


def solution(mesh):
    placed = (P(("row", "col"), None), P("row", "col"), P("row", "col"), P(), P(), P())
    return jax.shard_map(
        functools.partial(shards, (mesh.shape["row"], mesh.shape["col"])),
        mesh=mesh, in_specs=placed, out_specs=P(("row", "col"), None), check_vma=False,
    )
```

time: 72.9 us -> 67.3 us (0.923)
  Pallas kernels: 71.2 us -> 65.6 us
    pallas_call x1, Pallas kernels: 71.2 us -> 65.6 us  [shards(): pl.pallas_call(functools.partial(step_kernel, counts), name='gradient_ste...]
where the time goes in v2:
time: 67.3 us; the launch traced here: 67.2 us
  Pallas kernels  65.6 us (97%)
  local copies, waits for them, and re-layouts  1.57 us (2%)
    pallas_call x1, Pallas kernels, shards(): pl.pallas_call(functools.partial(step_kernel, counts), name='gradient_ste...  65.6 us
    unnamed x1, local copies, waits for them, and re-layouts  1.57 us

profile of v2, /device:TPU:1, one launch (start us, length us, event | category | flops | bytes accessed | tf_op | source)
XLA Modules:
  0.0 67.2 jit_solution(6798996680820498349)
XLA Ops:
  0.0 65.6 %gradient_step.1 = f32[32,1024]{1,0:T(8,128)} custom-call(f32[8]{0:T(128)} %weight.1, s32[4,32]{1,0:T(4,128)} %inst.1, f32[32,1024]{1,0:T(8,128)} %cells.1, f32[8,65]{1,0:T(8,128)} %row_taps.1, f32[8,65]{1,0:T(8,128)} %col_taps.1, f32[128,1024]{1,0:T(8,128)} %target_hbm.1), custom_call_target="tpu_custom_call" | custom-call | tf_op jit(solution)/shard_map/gradient_step/pallas_call | solution.py:459
  65.6 1.6 %copy.8 = f32[32,1024]{1,0:T(8,128)} copy(f32[32,1024]{1,0:T(8,128)} %gradient_step.1) | data formatting | bytes 262144

commit v3 on v2

--- a/solution.py
+++ b/solution.py
@@ -73,7 +73,7 @@
     return a, b, c, d
 
 
-def build_bands(row_taps, col_taps, a_own, a_halo, at_own, at_halo, b_both, bt_both, pad):
+def build_bands(row_taps, col_taps, a_own, a_halo, at_own, at_rim, b_both, bt_both, pad):
     pad[...] = jnp.zeros_like(pad)
     pad[0:8, 0:TAPS] = row_taps[...]
     pad[8:16, 0:TAPS] = col_taps[...]
@@ -102,7 +102,9 @@
         a_own[rows, :] = own.astype(BF16)
         a_halo[rows, :] = halo.astype(BF16)
         at_own[:, rows] = own.T.astype(BF16)
-        at_halo[:, rows] = halo.T[0:128].astype(BF16)
+        turned = halo.T
+        for h in range(2):
+            at_rim[k, :, 128 * h:128 * h + 128] = turned[0:128].astype(BF16)
         for i, part in enumerate(split(shifted(8 + k))):
             part = part.astype(F32)
             lanes = pl.ds(i * 128, 128)
@@ -176,47 +178,71 @@
         power[...] = share if k == 0 else power[...] + share
 
 
-def adjoint_columns(weight, target, bt_both, fields, power, p_hi, p_lo, q_hi, q_lo):
+def products(weight, target, fields, power, p_hi, p_lo):
     for n in range(8):
         part = pl.ds(128 * n, 128)
         wanted = target[:, part]
         resist = 1.0 / (1.0 + jnp.exp(-STEEPNESS * (power[part, :] - THRESHOLD)))
         power[part, :] = (2.0 * STEEPNESS * 2.0) * (resist - wanted) * resist * (1.0 - resist)
     for k in range(KERNELS):
-        high, low = p_hi.at[k % 2], p_lo.at[k % 2]
         product = weight[k] * power[...] * fields[k]
-        high[1:9], low[1:9] = (v.reshape(8, 128, 128) for v in split(product))
-
+        p_hi[k, 1:9], p_lo[k, 1:9] = (v.reshape(8, 128, 128) for v in split(product))
+
+
+def windows(ref, start, count):
+    rows = count * ref.shape[1]
+    return jnp.concatenate(
+        [ref[start:start + count].reshape(rows, 128), ref[start + 1:start + 1 + count].reshape(rows, 128)], axis=1
+    )
+
+
+def adjoint_rim(at_rim, bt_both, p_hi, p_lo, z_hi, z_lo):
+    total = jnp.zeros((64 * GROUPS, 128), F32)
+    for k in range(KERNELS):
+        high, low = z_hi.at[k % 2], z_lo.at[k % 2]
+        for n in (1, 3, 5, 7):
+            upper = jnp.concatenate([p_hi[k, n], p_hi[k, n + 1]], axis=1)
+            lower = jnp.concatenate([p_lo[k, n], p_lo[k, n + 1]], axis=1)
+            both = mm(at_rim[k], jnp.concatenate([upper, lower], axis=0))
+            value = both[0:64] + both[64:128]
+            for h in range(2):
+                high[n + h], low[n + h] = split(value[:, 128 * h:128 * h + 128])
+        both = mm(windows(high, 0, GROUPS), bt_both[k])
+        total = total + both[:, :128] + both[:, 128:] + mm(windows(low, 0, GROUPS), bt_both[k, :, 0:128])
+    tiles = []
+    for g in range(GROUPS):
+        tiles += as_tiles(total[64 * g:64 * g + 64], g)
+    return tiles
+
+
+def as_tiles(value, g):
+    value = value.reshape(value.shape[0] // 32, 32, 128)
+    turned = swap_blocks([value[:, 8 * s:8 * s + 8] for s in range(4)])
+    return [(4 * g + q, turned[q]) for q in range(4)]
+
+
+def adjoint_columns(bt_both, p_hi, p_lo, q_hi, q_lo, groups):
+    for k in range(KERNELS):
         def window(ref):
-            return jnp.concatenate(
-                [ref[0:9].reshape(1152, 128), ref[1:10].reshape(1152, 128)], axis=1
-            )
-        both = mm(window(high), bt_both[k])
-        value = both[:, :128] + both[:, 128:] + mm(window(low), bt_both[k, :, 0:128])
+            return jnp.concatenate([windows(ref.at[k], start, count) for start, count in groups], axis=0)
+        both = mm(window(p_hi), bt_both[k])
+        value = both[:, :128] + both[:, 128:] + mm(window(p_lo), bt_both[k, :, 0:128])
         high, low = split(value)
-        for g in range(GROUPS):
-            rows = pl.ds(k * 128, 128)
-            q_hi[rows, lanes_of(g)] = high[128 * g:128 * g + 128]
-            q_lo[rows, lanes_of(g)] = low[128 * g:128 * g + 128]
-
-
-def adjoint_rows(bands, count, g, q_hi, q_lo):
-    tiles = []
-    if g == GROUPS - 1:
-        lanes = lanes_of(g)
+        rows = pl.ds(k * 128, 128)
+        for i, g in enumerate(g for start, count in groups for g in range(start, start + count)):
+            q_hi[rows, lanes_of(g)] = high[128 * i:128 * i + 128]
+            q_lo[rows, lanes_of(g)] = low[128 * i:128 * i + 128]
+
+
+def adjoint_rows(bands, g, count, q_hi, q_lo):
+    lanes = lanes_of(g, count)
+    if count == 1:
         both = mm(bands[...], jnp.concatenate([q_hi[:, lanes], q_lo[:, lanes]], axis=1))
         both = both[:, 0:128] + both[:, 128:256]
-        parts = [both[0:count] + both[count:2 * count]]
-    else:
-        lanes = lanes_of(g, 2)
-        both = mm(bands[...], q_hi[:, lanes])
-        value = both[0:count] + both[count:2 * count] + mm(bands[0:count, :], q_lo[:, lanes])
-        parts = [value[:, 0:128], value[:, 128:256]]
-    for h, value in enumerate(parts):
-        value = value.reshape(count // 32, 32, 128)
-        turned = swap_blocks([value[:, 8 * s:8 * s + 8] for s in range(4)])
-        tiles += [(4 * (g + h) + q, turned[q]) for q in range(4)]
-    return tiles
+        return as_tiles(both[0:128] + both[128:256], g)
+    both = mm(bands[...], q_hi[:, lanes])
+    value = both[0:128] + both[128:256] + mm(bands[0:128, :], q_lo[:, lanes])
+    return as_tiles(value[:, 0:128], g) + as_tiles(value[:, 128:256], g + 1)
 
 
 def exists(at, counts, step):
@@ -260,8 +286,8 @@
 def step_kernel(
     counts, weight, inst, cells, row_taps, col_taps, target_hbm, out,
     pad, table, cells3, outgoing, arrived, index_v, index_s, where_v, where_s, tile_v, tile_s, wide, target,
-    a_own, a_halo, at_own, at_halo, b_both, bt_both, taps_pad,
-    x_own, x_low, x_halo, early, y_hi, y_lo, fields, power, p_hi, p_lo, q_hi, q_lo,
+    a_own, a_halo, at_own, at_rim, b_both, bt_both, taps_pad,
+    x_own, x_low, x_halo, early, y_hi, y_lo, fields, power, p_hi, p_lo, z_hi, z_lo, q_hi, q_lo,
     rim_row, rim_col, halo_row, halo_col, halo_corner, own, back,
     table_send, table_recv, block_send, block_recv, cell_send, cell_recv, grad_send, grad_recv,
     halo_send, halo_recv, rim_send, rim_recv, local,
@@ -379,11 +405,15 @@
     where_copy.wait()
     tile_copy.wait()
     target_copy.wait()
-    build_bands(row_taps, col_taps, a_own, a_halo, at_own, at_halo, b_both, bt_both, taps_pad)
+    build_bands(row_taps, col_taps, a_own, a_halo, at_own, at_rim, b_both, bt_both, taps_pad)
     for ref in (p_hi, p_lo):
+        for k in range(KERNELS):
+            ref[k, 0] = jnp.zeros((128, 128), BF16)
+            ref[k, 9] = jnp.zeros((128, 128), BF16)
+    for ref in (z_hi, z_lo):
         for parity in range(2):
-            ref[parity, 0] = jnp.zeros((128, 128), BF16)
-            ref[parity, 9] = jnp.zeros((128, 128), BF16)
+            ref[parity, 0] = jnp.zeros((64, 128), BF16)
+            ref[parity, 9] = jnp.zeros((64, 128), BF16)
     everyone_wait(arrived, cell_send, cell_recv)
 
     def put(t, carry):
@@ -402,7 +432,7 @@
     wait_copies(halo, at, counts)
 
     forward(weight, wide, a_own, a_halo, b_both, x_own, x_low, x_halo, early, y_hi, y_lo, fields, power)
-    adjoint_columns(weight, target, bt_both, fields, power, p_hi, p_lo, q_hi, q_lo)
+    products(weight, target, fields, power, p_hi, p_lo)
 
     def rim(i, dr, dc):
         side_row, side_col = int(dr > 0), 0 if dc < 0 else TILE_COLS + 1
@@ -414,19 +444,24 @@
             source, landing = rim_row.at[side_row, side_col], halo_corner.at[2 * side_row + int(dc > 0)]
         return remote(source, landing, rim_send.at[i], rim_recv.at[i], (row + dr, col + dc))
 
-    for g in (0, 2, 4, 6, 8):
-        for c, tiles in adjoint_rows(at_halo, 64, g, q_hi, q_lo):
-            rim_row[:, c] = tiles
+    for c, tiles in adjoint_rim(at_rim, bt_both, p_hi, p_lo, z_hi, z_lo):
+        rim_row[:, c] = tiles
     start_copies(rim, at, counts, ACROSS)
-    for g in (0, 8, 2, 4, 6):
-        for c, tiles in adjoint_rows(at_own, 128, g, q_hi, q_lo):
+
+    def keep_own(g, count):
+        for c, tiles in adjoint_rows(at_own, g, count, q_hi, q_lo):
             if c in (0, TILE_COLS + 1):
                 rim_col[int(c > 0)] = tiles
             elif c <= TILE_COLS:
                 for a in range(TILE_ROWS):
                     own[TILE_COLS * a + c - 1] = tiles[a]
-        if g == 8:
-            start_copies(rim, at, counts, ALONG)
+    adjoint_columns(bt_both, p_hi, p_lo, q_hi, q_lo, ((0, 1), (8, 1)))
+    keep_own(0, 1)
+    keep_own(8, 1)
+    start_copies(rim, at, counts, ALONG)
+    adjoint_columns(bt_both, p_hi, p_lo, q_hi, q_lo, ((1, 7),))
+    for g, count in ((1, 2), (3, 2), (5, 2), (7, 1)):
+        keep_own(g, count)
     wait_copies(rim, at, counts)
     own[96:128] = own[96:128] + halo_row[0]
     own[0:32] = own[0:32] + halo_row[1]
@@ -467,13 +502,14 @@
             vmem((SLOTS, 8, 128), F32), vmem((256, 8, 128), F32), vmem((256, 8, 128), F32),
             vmem((2, 128), I32), smem((2, 128), I32), vmem((1, 128), I32), smem((1, 128), I32),
             vmem((2, 128), I32), smem((2, 128), I32), vmem((6, WIDE, 8, 128), F32), vmem((ROWS, COLS), F32),
-            vmem((1024, 256), BF16), vmem((1024, 256), BF16), vmem((256, 1024), BF16), vmem((128, 1024), BF16),
+            vmem((1024, 256), BF16), vmem((1024, 256), BF16), vmem((256, 1024), BF16), vmem((8, 128, 256), BF16),
             vmem((8, 256, 256), BF16), vmem((8, 256, 256), BF16), vmem((16, 256), F32),
             vmem((256, 1152), BF16), vmem((128, 1152), BF16), vmem((256, 1152), BF16),
             vmem((3, 1024, 256), F32),
             vmem((8, 9, 128, 128), BF16), vmem((8, 9, 128, 128), BF16),
             vmem((8, 1024, 128), F32), vmem((1024, 128), F32),
-            vmem((2, 10, 128, 128), BF16), vmem((2, 10, 128, 128), BF16),
+            vmem((8, 10, 128, 128), BF16), vmem((8, 10, 128, 128), BF16),
+            vmem((2, 10, 64, 128), BF16), vmem((2, 10, 64, 128), BF16),
             vmem((1024, 1152), BF16), vmem((1024, 1152), BF16),
             vmem((2, WIDE, 8, 128), F32), vmem((2, 4, 8, 128), F32),
             vmem((2, 32, 8, 128), F32), vmem((2, 4, 8, 128), F32), vmem((4, 8, 128), F32),

time: 67.3 us -> 66.4 us (0.987)
  Pallas kernels: 65.6 us -> 64.6 us
    pallas_call x1, Pallas kernels: 65.6 us -> 64.6 us  [shards(): pl.pallas_call(functools.partial(step_kernel, counts), name='gradient_ste...]
where the time goes in v3:
time: 66.4 us; the launch traced here: 66.2 us
  Pallas kernels  64.6 us (97%)
  local copies, waits for them, and re-layouts  1.57 us (2%)
    pallas_call x1, Pallas kernels, shards(): pl.pallas_call(functools.partial(step_kernel, counts), name='gradient_ste...  64.6 us
    unnamed x1, local copies, waits for them, and re-layouts  1.57 us

profile of v3, /device:TPU:1, one launch (start us, length us, event | category | flops | bytes accessed | tf_op | source)
XLA Modules:
  0.0 66.2 jit_solution(15056923155412183894)
XLA Ops:
  0.0 64.6 %gradient_step.1 = f32[32,1024]{1,0:T(8,128)} custom-call(f32[8]{0:T(128)} %weight.1, s32[4,32]{1,0:T(4,128)} %inst.1, f32[32,1024]{1,0:T(8,128)} %cells.1, f32[8,65]{1,0:T(8,128)} %row_taps.1, f32[8,65]{1,0:T(8,128)} %col_taps.1, f32[128,1024]{1,0:T(8,128)} %target_hbm.1), custom_call_target="tpu_custom_call" | custom-call | tf_op jit(solution)/shard_map/gradient_step/pallas_call | solution.py:494
  64.7 1.6 %copy.8 = f32[32,1024]{1,0:T(8,128)} copy(f32[32,1024]{1,0:T(8,128)} %gradient_step.1) | data formatting | bytes 262144

commit v4 on v3

--- a/solution.py
+++ b/solution.py
@@ -73,7 +73,11 @@
     return a, b, c, d
 
 
-def build_bands(row_taps, col_taps, a_own, a_halo, at_own, at_rim, b_both, bt_both, pad):
+def lanes_of(g, count=1):
+    return pl.ds(g * 128, 128 * count)
+
+
+def build_bands(weight, row_taps, col_taps, a_own, a_halo, at_own, at_rim, b_both, bt_both, pad):
     pad[...] = jnp.zeros_like(pad)
     pad[0:8, 0:TAPS] = row_taps[...]
     pad[8:16, 0:TAPS] = col_taps[...]
@@ -105,16 +109,13 @@
         turned = halo.T
         for h in range(2):
             at_rim[k, :, 128 * h:128 * h + 128] = turned[0:128].astype(BF16)
-        for i, part in enumerate(split(shifted(8 + k))):
-            part = part.astype(F32)
-            lanes = pl.ds(i * 128, 128)
-            b_both[k, :, lanes] = part.T.astype(BF16)
-            bt_both[k, 0:128, lanes] = part[:, 128:256].astype(BF16)
-            bt_both[k, 128:256, lanes] = part[:, 0:128].astype(BF16)
-
-
-def lanes_of(g, count=1):
-    return pl.ds(g * 128, 128 * count)
+        root = jnp.sqrt(jnp.full((1, 256), weight[k], F32))
+        band = shifted(8 + k) * root
+        for i, part in enumerate(split(band)):
+            b_both[k, :, lanes_of(i)] = part.astype(F32).T.astype(BF16)
+        for i, part in enumerate(split(band * (4.0 * STEEPNESS))):
+            bt_both[k, 0:128, lanes_of(i)] = part[:, 128:256]
+            bt_both[k, 128:256, lanes_of(i)] = part[:, 0:128]
 
 
 EARLY = (1, 3, 5)
@@ -137,7 +138,7 @@
     mask_own(7, wide, x_own, x_low)
 
 
-def forward(weight, wide, a_own, a_halo, b_both, x_own, x_low, x_halo, early, y_hi, y_lo, fields, power):
+def forward_rows(wide, a_own, a_halo, x_own, x_low, x_halo, early, y_hi, y_lo):
     for g in (0, 8):
         mask_own(g, wide, x_own, x_low)
     x_halo[192:256, :] = jnp.zeros((64, GROUPS * 128), BF16)
@@ -166,27 +167,23 @@
         value = early[i] + mm(a_halo[...], x_halo[:, lanes_of(g, 2)])
         for h in range(2):
             keep(g + h, value[:, 128 * h:128 * h + 128])
-    for k in range(KERNELS):
-        def window(ref):
-            return jnp.concatenate(
-                [ref[k, 0:8].reshape(1024, 128), ref[k, 1:9].reshape(1024, 128)], axis=1
-            )
-        both = mm(window(y_hi), b_both[k])
-        field = both[:, :128] + both[:, 128:] + mm(window(y_lo), b_both[k, :, 0:128])
-        fields[k] = field
-        share = weight[k] * field * field
-        power[...] = share if k == 0 else power[...] + share
-
-
-def products(weight, target, fields, power, p_hi, p_lo):
-    for n in range(8):
-        part = pl.ds(128 * n, 128)
-        wanted = target[:, part]
-        resist = 1.0 / (1.0 + jnp.exp(-STEEPNESS * (power[part, :] - THRESHOLD)))
-        power[part, :] = (2.0 * STEEPNESS * 2.0) * (resist - wanted) * resist * (1.0 - resist)
-    for k in range(KERNELS):
-        product = weight[k] * power[...] * fields[k]
-        p_hi[k, 1:9], p_lo[k, 1:9] = (v.reshape(8, 128, 128) for v in split(product))
+
+
+def image(target, b_both, y_hi, y_lo, fields, p_hi, p_lo):
+    for n in range(0, 8, 2):
+        part = pl.ds(128 * n, 256)
+        intensity = None
+        for k in range(KERNELS):
+            both = mm(windows(y_hi.at[k], n, 2), b_both[k])
+            field = both[:, :128] + both[:, 128:] + mm(windows(y_lo.at[k], n, 2), b_both[k, :, 0:128])
+            fields[k, part] = field
+            intensity = field * field if k == 0 else intensity + field * field
+        wanted = jnp.concatenate([target[:, lanes_of(n)], target[:, lanes_of(n + 1)]], axis=0)
+        resist = 1.0 / (1.0 + jnp.exp(-STEEPNESS * (intensity - THRESHOLD)))
+        sensitivity = (resist - wanted) * resist * (1.0 - resist)
+        for k in range(KERNELS):
+            parts = split(sensitivity * fields[k, part])
+            p_hi[k, n + 1:n + 3], p_lo[k, n + 1:n + 3] = (v.reshape(2, 128, 128) for v in parts)
 
 
 def windows(ref, start, count):
@@ -287,7 +284,7 @@
     counts, weight, inst, cells, row_taps, col_taps, target_hbm, out,
     pad, table, cells3, outgoing, arrived, index_v, index_s, where_v, where_s, tile_v, tile_s, wide, target,
     a_own, a_halo, at_own, at_rim, b_both, bt_both, taps_pad,
-    x_own, x_low, x_halo, early, y_hi, y_lo, fields, power, p_hi, p_lo, z_hi, z_lo, q_hi, q_lo,
+    x_own, x_low, x_halo, early, y_hi, y_lo, fields, p_hi, p_lo, z_hi, z_lo, q_hi, q_lo,
     rim_row, rim_col, halo_row, halo_col, halo_corner, own, back,
     table_send, table_recv, block_send, block_recv, cell_send, cell_recv, grad_send, grad_recv,
     halo_send, halo_recv, rim_send, rim_recv, local,
@@ -405,7 +402,7 @@
     where_copy.wait()
     tile_copy.wait()
     target_copy.wait()
-    build_bands(row_taps, col_taps, a_own, a_halo, at_own, at_rim, b_both, bt_both, taps_pad)
+    build_bands(weight, row_taps, col_taps, a_own, a_halo, at_own, at_rim, b_both, bt_both, taps_pad)
     for ref in (p_hi, p_lo):
         for k in range(KERNELS):
             ref[k, 0] = jnp.zeros((128, 128), BF16)
@@ -431,8 +428,8 @@
     rows_own(wide, a_own, x_own, x_low, early)
     wait_copies(halo, at, counts)
 
-    forward(weight, wide, a_own, a_halo, b_both, x_own, x_low, x_halo, early, y_hi, y_lo, fields, power)
-    products(weight, target, fields, power, p_hi, p_lo)
+    forward_rows(wide, a_own, a_halo, x_own, x_low, x_halo, early, y_hi, y_lo)
+    image(target, b_both, y_hi, y_lo, fields, p_hi, p_lo)
 
     def rim(i, dr, dc):
         side_row, side_col = int(dr > 0), 0 if dc < 0 else TILE_COLS + 1
@@ -507,7 +504,7 @@
             vmem((256, 1152), BF16), vmem((128, 1152), BF16), vmem((256, 1152), BF16),
             vmem((3, 1024, 256), F32),
             vmem((8, 9, 128, 128), BF16), vmem((8, 9, 128, 128), BF16),
-            vmem((8, 1024, 128), F32), vmem((1024, 128), F32),
+            vmem((8, 1024, 128), F32),
             vmem((8, 10, 128, 128), BF16), vmem((8, 10, 128, 128), BF16),
             vmem((2, 10, 64, 128), BF16), vmem((2, 10, 64, 128), BF16),
             vmem((1024, 1152), BF16), vmem((1024, 1152), BF16),

time: 66.4 us -> 66.1 us (level)
  no operation moved by 1% of the time
where the time goes in v4:
time: 66.1 us; the launch traced here: 66 us
  Pallas kernels  64.4 us (97%)
  local copies, waits for them, and re-layouts  1.57 us (2%)
    pallas_call x1, Pallas kernels, shards(): pl.pallas_call(functools.partial(step_kernel, counts), name='gradient_ste...  64.4 us
    unnamed x1, local copies, waits for them, and re-layouts  1.57 us

profile of v4, /device:TPU:1, one launch (start us, length us, event | category | flops | bytes accessed | tf_op | source)
XLA Modules:
  0.0 66.0 jit_solution(2565480062806639840)
XLA Ops:
  0.0 64.4 %gradient_step.1 = f32[32,1024]{1,0:T(8,128)} custom-call(f32[8]{0:T(128)} %weight.1, s32[4,32]{1,0:T(4,128)} %inst.1, f32[32,1024]{1,0:T(8,128)} %cells.1, f32[8,65]{1,0:T(8,128)} %row_taps.1, f32[8,65]{1,0:T(8,128)} %col_taps.1, f32[128,1024]{1,0:T(8,128)} %target_hbm.1), custom_call_target="tpu_custom_call" | custom-call | tf_op jit(solution)/shard_map/gradient_step/pallas_call | solution.py:491
  64.4 1.6 %copy.8 = f32[32,1024]{1,0:T(8,128)} copy(f32[32,1024]{1,0:T(8,128)} %gradient_step.1) | data formatting | bytes 262144
